TPU v7x, 128 devices: a whole 4x4x4 slice. The times are simulated.
128 devices in a mesh: fluid: 32 (over x, y, core), solid: 4 (over z).
Axes of the slice: x: 4, y: 4, z: 4, core: 2. Of those that a mesh axis runs over, the one named last changes fastest.
Arguments:
- rbf_blocks: bfloat16 [13312, 256, 256], P(('fluid', 'solid')), may hold values from -0.375 to 0.375
- fluid_traction: bfloat16 [13312, 768], P(('fluid', 'solid')), may hold values from -24 to 24
- fluid_mass: bfloat16 [13312, 768], P(('fluid', 'solid')), may hold values from 0.19921875 to 2
- route: int32 [13312, 1], P(('fluid', 'solid')), may hold values from 0 to 127; in each aligned block of 104 rows (0 to 103, 104 to 207, ...) at most 2 rows name the same one
- slot: int32 [13312], P(('fluid', 'solid')), may hold values from 0 to 7
- shell_inverse: bfloat16 [1024, 768, 768], P(('fluid', 'solid')), may hold values from -0.0078125 to 0.0078125
- robin_coef: float32 [1024, 768], P(('fluid', 'solid')), may hold values from 1 to 27
- shell_start: float32 [1024, 768], P(('fluid', 'solid')), may hold values from -3 to 3
Outputs:
- shell_displacement: float32 [1024, 768], P(('fluid', 'solid'))
- fluid_load: bfloat16 [13312, 768], P(('fluid', 'solid'))
- residual_norms: float32 [6], replicated
Inputs may be any that keep to these rules, and one draw needn't show every extreme that they name: `route`: among the 104 blocks of one device at most 2 name the same owner device.
All inputs are finite; a program needn't handle non-finite values.
Results may differ from a plain program's by a relative error of at most 0.009.
Values may be sent and summed in bfloat16 or wider, within the bound.
No kernel may reach another device: no remote copies, remote signals or barrier semaphores. Data moves between devices by JAX's collectives and lax.ppermute only.
A program may use at most 128 MiB of HBM per device.

v0:
```python
import jax
import jax.numpy as jnp
from jax import lax
from jax.sharding import Mesh
from jax.sharding import PartitionSpec as P

ITERS = 6
FLUID_SOLID = ("fluid_0", "fluid_1", "fluid_2", "solid")
FLUID = ("fluid_0", "fluid_1", "fluid_2")
RELAX = 0.3
EPSILON = 1e-06


def over_axes(array, axes):
    for axis in axes:
        array = lax.psum(array, axis)
    return array


def transport(buffer, devices, capacity):
    breadth = buffer.shape[1]
    moved = lax.all_to_all(
        buffer.reshape(devices, capacity, breadth),
        FLUID_SOLID,
        split_axis=0,
        concat_axis=0,
        tiled=True,
    )
    return moved.reshape(devices * capacity, breadth)


def least_squares(gram, target_side):
    order = gram.shape[0]
    lower = [[None] * order for _ in range(order)]
    for row in range(order):
        for column in range(row + 1):
            total = gram[row, column]
            for inner in range(column):
                total = total - lower[row][inner] * lower[column][inner]
            if row == column:
                lower[row][row] = jnp.sqrt(total)
            else:
                lower[row][column] = total / lower[column][column]
    middle = []
    for row in range(order):
        total = target_side[row]
        for inner in range(row):
            total = total - lower[row][inner] * middle[inner]
        middle.append(total / lower[row][row])
    result = [None] * order
    for row in reversed(range(order)):
        total = middle[row]
        for inner in range(row + 1, order):
            total = total - lower[inner][row] * result[inner]
        result[row] = total / lower[row][row]
    return jnp.stack(result)


def per_device(
    rbf_blocks, fluid_traction, fluid_mass, route, slot, shell_inverse, robin_coef, shell_start
):
    devices = lax.axis_size(FLUID) * lax.axis_size("solid")
    blocks = rbf_blocks.shape[0]
    nodes = rbf_blocks.shape[1]
    breadth = 3 * nodes
    shells = shell_inverse.shape[0]
    capacity = max(2, 2 * blocks // devices)
    slots_all = devices * capacity
    destination = route[:, 0]
    block_order = jnp.arange(blocks, dtype=jnp.int32)
    earlier = (destination[:, None] == destination[None, :]) & (
        block_order[None, :] < block_order[:, None]
    )
    slot_rank = jnp.sum(earlier.astype(jnp.int32), axis=1)
    position = destination * capacity + slot_rank
    positions = jnp.arange(slots_all, dtype=jnp.int32)
    placing = positions[:, None] == position[None, :]
    place_out = placing.astype(jnp.bfloat16)
    place_in = (position[:, None] == positions[None, :]).astype(jnp.bfloat16)
    wanted = jnp.max(jnp.where(placing, slot[None, :] + 1, 0), axis=1) - 1
    asked = lax.all_to_all(
        wanted.reshape(devices, capacity), FLUID_SOLID, split_axis=0, concat_axis=0, tiled=True
    ).reshape(slots_all)
    shell_ids = jnp.arange(shells, dtype=jnp.int32)
    picking = (asked[:, None] == shell_ids[None, :]).astype(jnp.bfloat16)
    collecting = (shell_ids[:, None] == asked[None, :]).astype(jnp.bfloat16)
    traction = fluid_traction.astype(jnp.float32)
    massive = fluid_mass.astype(jnp.float32)
    count = shells * devices * breadth
    current = shell_start
    residuals = []
    images = []
    norms = []
    last_load = None
    for iteration in range(ITERS):
        current_half = current.astype(jnp.bfloat16)
        outgoing = jnp.dot(picking, current_half, preferred_element_type=jnp.float32).astype(
            jnp.bfloat16
        )
        incoming = transport(outgoing, devices, capacity)
        displaced = jnp.dot(place_in, incoming, preferred_element_type=jnp.float32).astype(
            jnp.bfloat16
        )
        moved = jnp.einsum(
            "bcj,bij->bci",
            displaced.reshape(blocks, 3, nodes),
            rbf_blocks,
            preferred_element_type=jnp.float32,
        ).reshape(blocks, breadth)
        load = (traction - massive * moved).astype(jnp.bfloat16)
        last_load = load
        mapped = (
            jnp.einsum(
                "bci,bij->bcj",
                load.reshape(blocks, 3, nodes),
                rbf_blocks,
                preferred_element_type=jnp.float32,
            )
            .reshape(blocks, breadth)
            .astype(jnp.bfloat16)
        )
        sending = jnp.dot(place_out, mapped, preferred_element_type=jnp.float32).astype(
            jnp.bfloat16
        )
        arrived = transport(sending, devices, capacity)
        shell_load = jnp.dot(collecting, arrived, preferred_element_type=jnp.float32)
        forcing = (shell_load + robin_coef * current).astype(jnp.bfloat16)
        image = jnp.einsum("bi,bij->bj", forcing, shell_inverse, preferred_element_type=jnp.float32)
        residual = image - current
        residuals.append(residual)
        images.append(image)
        squares_local = jnp.sum(residual * residual)
        if iteration == 0:
            gram_local = jnp.zeros((1, 1), jnp.float32)
            rhs_local = jnp.zeros((1,), jnp.float32)
        else:
            changes = jnp.stack(
                [(residuals[i + 1] - residuals[i]).reshape(-1) for i in range(iteration)]
            )
            gram_local = jnp.dot(changes, changes.T, precision=lax.Precision.HIGHEST)
            rhs_local = jnp.dot(changes, residual.reshape(-1), precision=lax.Precision.HIGHEST)
        gram, rhs, squares = (
            over_axes(gram_local, FLUID_SOLID),
            over_axes(rhs_local, FLUID_SOLID),
            over_axes(squares_local, FLUID_SOLID),
        )
        norms.append(jnp.sqrt(squares / count + EPSILON))
        if iteration == 0:
            current = current + RELAX * residual
        else:
            image_changes = jnp.stack([images[i + 1] - images[i] for i in range(iteration)])
            coefs = least_squares(gram, -rhs)
            current = image + jnp.tensordot(
                coefs, image_changes, axes=1, precision=lax.Precision.HIGHEST
            )
    return (current, last_load, jnp.stack(norms))


def solution(mesh):
    split = Mesh(
        mesh.devices.reshape(4, 4, 2, mesh.shape["solid"]),
        ("fluid_0", "fluid_1", "fluid_2", "solid"),
    )
    placed = (
        P(FLUID_SOLID, None, None),
        P(FLUID_SOLID, None),
        P(FLUID_SOLID, None),
        P(FLUID_SOLID, None),
        P(FLUID_SOLID),
        P(FLUID_SOLID, None, None),
        P(FLUID_SOLID, None),
        P(FLUID_SOLID, None),
    )
    return jax.shard_map(
        per_device,
        mesh=split,
        in_specs=placed,
        out_specs=(P(FLUID_SOLID, None), P(FLUID_SOLID, None), P()),
        check_vma=False,
    )
```

profile of v0, /device:TPU:0, one launch (start us, length us, event | category | flops | bytes accessed | tf_op | source)
XLA Modules:
  0.0 566.7 jit_solution(6310580616104771973)
XLA Ops:
  2.5 20.0 %all_to_all.66 = s32[128,1,2]{2,1,0:T(1,128)S(1)} all-to-all(s32[128,1,2]{2,1,0:T(1,128)S(1)} %bitcast.371), channel_id=1, replica_groups=mesh['fluid_0'=4,'fluid_1'=4,'fluid_2'=2,'solid'=4] {'fluid_0','fluid_1'..., dimensions={0} | all-to-all | bytes 2048 | tf_op jit(solution)/shard_map/all_to_all | solution.py:81
  33.7 9.0 %all-to-all-done.1 = bf16[128,2,768]{2,1,0:T(2,128)(2,1)S(1)} async-done(((bf16[128,2,768]{2,1,0:T(2,128)(2,1)}), bf16[128,2,768]{2,1,0:T(2,128)(2,1)S(1)}, u32[]{:S(2)}, u32[]{:S(2)}) %all-to-all-start.1) | async-done | bytes 393248 | tf_op jit(solution)/shard_map/all_to_all | solution.py:22
  59.9 16.5 %all_to_all.67 = bf16[128,2,768]{2,1,0:T(2,128)(2,1)S(1)} all-to-all(bf16[128,2,768]{2,1,0:T(2,128)(2,1)S(1)} %reshape.214), channel_id=1, replica_groups=mesh['fluid_0'=4,'fluid_1'=4,'fluid_2'=2,'solid'=4] {'fluid_0','fluid_1'..., dimensions={0} | all-to-all | bytes 786432 | tf_op jit(solution)/shard_map/all_to_all | solution.py:22
  82.3 16.7 %all_to_all.68 = bf16[128,2,768]{2,1,0:T(2,128)(2,1)S(1)} all-to-all(bf16[128,2,768]{2,1,0:T(2,128)(2,1)S(1)} %reshape.216), channel_id=1, replica_groups=mesh['fluid_0'=4,'fluid_1'=4,'fluid_2'=2,'solid'=4] {'fluid_0','fluid_1'..., dimensions={0} | all-to-all | bytes 786432 | tf_op jit(solution)/shard_map/all_to_all | solution.py:22
  116.2 16.5 %all_to_all.69 = bf16[128,2,768]{2,1,0:T(2,128)(2,1)S(1)} all-to-all(bf16[128,2,768]{2,1,0:T(2,128)(2,1)S(1)} %reshape.221), channel_id=1, replica_groups=mesh['fluid_0'=4,'fluid_1'=4,'fluid_2'=2,'solid'=4] {'fluid_0','fluid_1'..., dimensions={0} | all-to-all | bytes 786432 | tf_op jit(solution)/shard_map/all_to_all | solution.py:22
  138.7 9.5 %all-reduce.14 = (f32[1]{0:T(128)}, f32[1,1]{1,0:T(1,128)}) all-reduce(f32[1]{0:T(128)} %bitcast.16, f32[1,1]{1,0:T(1,128)} %bitcast.18), channel_id=1, replica_groups=mesh['fluid_0'=4,'fluid_1'=4,'fluid_2'=2,'solid'=4] {'fluid_0'}, use_global_device_ids=true, to_apply=%region_2.3 | all-reduce | flops 2 | bytes 16 | tf_op jit(solution)/shard_map/psum | solution.py:16
  148.2 9.6 %all-reduce.9 = (f32[1]{0:T(128)}, f32[1,1]{1,0:T(1,128)}) all-reduce(f32[1]{0:T(128)} %get-tuple-element.62, f32[1,1]{1,0:T(1,128)} %get-tuple-element.63), channel_id=1, replica_groups=mesh['fluid_0'=4,'fluid_1'=4,'fluid_2'=2,'solid'=4] {'fluid_1'}, use_global_device_ids=true, to_apply=%region_3.4 | all-reduce | flops 2 | bytes 16 | tf_op jit(solution)/shard_map/psum | solution.py:16
  160.9 9.2 %all-reduce.4 = (f32[1]{0:T(128)}, f32[1,1]{1,0:T(1,128)}) all-reduce(f32[1]{0:T(128)} %get-tuple-element.78, f32[1,1]{1,0:T(1,128)} %get-tuple-element.79), channel_id=1, replica_groups=mesh['fluid_0'=4,'fluid_1'=4,'fluid_2'=2,'solid'=4] {'solid'}, use_global_device_ids=true, to_apply=%region_5.6 | all-reduce | flops 2 | bytes 16 | tf_op jit(solution)/shard_map/psum | solution.py:16
  172.0 16.3 %all_to_all.70 = bf16[128,2,768]{2,1,0:T(2,128)(2,1)S(1)} all-to-all(bf16[128,2,768]{2,1,0:T(2,128)(2,1)S(1)} %reshape.224), channel_id=1, replica_groups=mesh['fluid_0'=4,'fluid_1'=4,'fluid_2'=2,'solid'=4] {'fluid_0','fluid_1'..., dimensions={0} | all-to-all | bytes 786432 | tf_op jit(solution)/shard_map/all_to_all | solution.py:22
  211.0 11.9 %all-to-all-done.6 = bf16[128,2,768]{2,1,0:T(2,128)(2,1)S(1)} async-done(((bf16[128,2,768]{2,1,0:T(2,128)(2,1)}), bf16[128,2,768]{2,1,0:T(2,128)(2,1)S(1)}, u32[]{:S(2)}, u32[]{:S(2)}) %all-to-all-start.6) | async-done | bytes 393248 | tf_op jit(solution)/shard_map/all_to_all | solution.py:22
  230.0 8.9 %all-reduce.13 = (f32[2]{0:T(128)S(1)}, f32[2,2]{1,0:T(2,128)S(1)}) all-reduce(f32[2]{0:T(128)S(1)} %convolution_bitcast_fusion.3, f32[2,2]{1,0:T(2,128)S(1)} %fusion.69), channel_id=1, replica_groups=mesh['fluid_0'=4,'fluid_1'=4,'fluid_2'=2,'solid'=4] {'fluid_0'}, use_global_device_ids=true, to_apply=%region_10.11 | all-reduce | flops 6 | bytes 48 | tf_op jit(solution)/shard_map/psum | solution.py:16
  238.9 9.0 %all-reduce.8 = (f32[2]{0:T(128)S(1)}, f32[2,2]{1,0:T(2,128)S(1)}) all-reduce(f32[2]{0:T(128)S(1)} %get-tuple-element.60, f32[2,2]{1,0:T(2,128)S(1)} %get-tuple-element.61), channel_id=1, replica_groups=mesh['fluid_0'=4,'fluid_1'=4,'fluid_2'=2,'solid'=4] {'fluid_1'}, use_global_device_ids=true, to_apply=%region_11.12 | all-reduce | flops 6 | bytes 48 | tf_op jit(solution)/shard_map/psum | solution.py:16
  264.3 16.0 %all_to_all.71 = bf16[128,2,768]{2,1,0:T(2,128)(2,1)S(1)} all-to-all(bf16[128,2,768]{2,1,0:T(2,128)(2,1)S(1)} %reshape.232), channel_id=1, replica_groups=mesh['fluid_0'=4,'fluid_1'=4,'fluid_2'=2,'solid'=4] {'fluid_0','fluid_1'..., dimensions={0} | all-to-all | bytes 786432 | tf_op jit(solution)/shard_map/all_to_all | solution.py:22
  297.6 16.5 %all_to_all.72 = bf16[128,2,768]{2,1,0:T(2,128)(2,1)S(1)} all-to-all(bf16[128,2,768]{2,1,0:T(2,128)(2,1)S(1)} %reshape.237), channel_id=1, replica_groups=mesh['fluid_0'=4,'fluid_1'=4,'fluid_2'=2,'solid'=4] {'fluid_0','fluid_1'..., dimensions={0} | all-to-all | bytes 786432 | tf_op jit(solution)/shard_map/all_to_all | solution.py:22
  321.2 8.9 %all-reduce.12 = (f32[3]{0:T(128)S(1)}, f32[3,3]{1,0:T(4,128)S(1)}) all-reduce(f32[3]{0:T(128)S(1)} %convolution_bitcast_fusion.2, f32[3,3]{1,0:T(4,128)S(1)} %fusion.49), channel_id=1, replica_groups=mesh['fluid_0'=4,'fluid_1'=4,'fluid_2'=2,'solid'=4] {'fluid_0'}, use_global_device_ids=true, to_apply=%region_18.19 | all-reduce | flops 12 | bytes 96 | tf_op jit(solution)/shard_map/psum | solution.py:16
  330.0 9.0 %all-reduce.7 = (f32[3]{0:T(128)S(1)}, f32[3,3]{1,0:T(4,128)S(1)}) all-reduce(f32[3]{0:T(128)S(1)} %get-tuple-element.58, f32[3,3]{1,0:T(4,128)S(1)} %get-tuple-element.59), channel_id=1, replica_groups=mesh['fluid_0'=4,'fluid_1'=4,'fluid_2'=2,'solid'=4] {'fluid_1'}, use_global_device_ids=true, to_apply=%region_19.20 | all-reduce | flops 12 | bytes 96 | tf_op jit(solution)/shard_map/psum | solution.py:16
  358.3 16.1 %all_to_all.73 = bf16[128,2,768]{2,1,0:T(2,128)(2,1)S(1)} all-to-all(bf16[128,2,768]{2,1,0:T(2,128)(2,1)S(1)} %reshape.240), channel_id=1, replica_groups=mesh['fluid_0'=4,'fluid_1'=4,'fluid_2'=2,'solid'=4] {'fluid_0','fluid_1'..., dimensions={0} | all-to-all | bytes 786432 | tf_op jit(solution)/shard_map/all_to_all | solution.py:22
  391.5 16.5 %all_to_all.74 = bf16[128,2,768]{2,1,0:T(2,128)(2,1)S(1)} all-to-all(bf16[128,2,768]{2,1,0:T(2,128)(2,1)S(1)} %reshape.245), channel_id=1, replica_groups=mesh['fluid_0'=4,'fluid_1'=4,'fluid_2'=2,'solid'=4] {'fluid_0','fluid_1'..., dimensions={0} | all-to-all | bytes 786432 | tf_op jit(solution)/shard_map/all_to_all | solution.py:22
  424.1 9.0 %all-reduce.6 = (f32[4]{0:T(128)S(1)}, f32[4,4]{1,0:T(4,128)S(1)}) all-reduce(f32[4]{0:T(128)S(1)} %get-tuple-element.56, f32[4,4]{1,0:T(4,128)S(1)} %get-tuple-element.57), channel_id=1, replica_groups=mesh['fluid_0'=4,'fluid_1'=4,'fluid_2'=2,'solid'=4] {'fluid_1'}, use_global_device_ids=true, to_apply=%region_27.28 | all-reduce | flops 20 | bytes 160 | tf_op jit(solution)/shard_map/psum | solution.py:16
  455.7 16.1 %all_to_all.75 = bf16[128,2,768]{2,1,0:T(2,128)(2,1)S(1)} all-to-all(bf16[128,2,768]{2,1,0:T(2,128)(2,1)S(1)} %reshape.248), channel_id=1, replica_groups=mesh['fluid_0'=4,'fluid_1'=4,'fluid_2'=2,'solid'=4] {'fluid_0','fluid_1'..., dimensions={0} | all-to-all | bytes 786432 | tf_op jit(solution)/shard_map/all_to_all | solution.py:22
  495.4 11.1 %all-to-all-done.12 = bf16[128,2,768]{2,1,0:T(2,128)(2,1)S(1)} async-done(((bf16[128,2,768]{2,1,0:T(2,128)(2,1)}), bf16[128,2,768]{2,1,0:T(2,128)(2,1)S(1)}, u32[]{:S(2)}, u32[]{:S(2)}) %all-to-all-start.12) | async-done | bytes 393248 | tf_op jit(solution)/shard_map/all_to_all | solution.py:22
  513.8 9.7 %all-reduce.10 = (f32[5]{0:T(128)S(1)}, f32[5,5]{1,0:T(8,128)S(1)}, f32[]{:T(128)}, f32[]{:T(128)}, f32[]{:T(128)}, /*index=5*/f32[]{:T(128)}, f32[]{:T(128)}, f32[]{:T(128)}) all-reduce(f32[5]{0:T(128)S(1)} %convolution_bitcast_fusion, ...), channel_id=1, replica_groups=mesh['fluid_0'=4,'fluid_1'=4,'fluid_2'=2,'solid'=4] {'fluid_0'}, use_global_device_ids=true, to_apply=%region_34.35 | all-reduce | flops 36 | bytes 288 | tf_op jit(solution)/shard_map/psum | solution.py:16
  523.5 9.8 %all-reduce.5 = (f32[5]{0:T(128)S(1)}, f32[5,5]{1,0:T(8,128)S(1)}, f32[]{:T(128)}, f32[]{:T(128)}, f32[]{:T(128)}, /*index=5*/f32[]{:T(128)}, f32[]{:T(128)}, f32[]{:T(128)}) all-reduce(f32[5]{0:T(128)S(1)} %get-tuple-element.48, ...), channel_id=1, replica_groups=mesh['fluid_0'=4,'fluid_1'=4,'fluid_2'=2,'solid'=4] {'fluid_1'}, use_global_device_ids=true, to_apply=%region_35.36 | all-reduce | flops 36 | bytes 288 | tf_op jit(solution)/shard_map/psum | solution.py:16
  536.5 9.4 %all-reduce = (f32[5]{0:T(128)S(1)}, f32[5,5]{1,0:T(8,128)S(1)}, f32[]{:T(128)}, f32[]{:T(128)}, f32[]{:T(128)}, /*index=5*/f32[]{:T(128)}, f32[]{:T(128)}, f32[]{:T(128)}) all-reduce(f32[5]{0:T(128)S(1)} %get-tuple-element.64, ...), channel_id=1, replica_groups=mesh['fluid_0'=4,'fluid_1'=4,'fluid_2'=2,'solid'=4] {'solid'}, use_global_device_ids=true, to_apply=%region_37.38 | all-reduce | flops 36 | bytes 288 | tf_op jit(solution)/shard_map/psum | solution.py:16
  (187 shorter events, 226.3 us)
Async XLA Ops:
  25.9 16.8 %all-to-all-start.1 = ((bf16[128,2,768]{2,1,0:T(2,128)(2,1)}), bf16[128,2,768]{2,1,0:T(2,128)(2,1)S(1)}, u32[]{:S(2)}, u32[]{:S(2)}) async-start(bf16[128,2,768]{2,1,0:T(2,128)(2,1)} %reshape.209), calls=%async_computation.1 | async-start | bytes 786432 | tf_op jit(solution)/shard_map/all_to_all | solution.py:22
  52.1 24.4 %copy-start = (f32[8,768]{1,0:T(8,128)S(1)}, f32[8,768]{1,0:T(8,128)}, u32[]{:S(2)}) copy-start(f32[8,768]{1,0:T(8,128)} %param.14) | copy-start | bytes 73732
  52.2 24.4 %copy-start.1 = (f32[8,768]{1,0:T(8,128)S(1)}, f32[8,768]{1,0:T(8,128)}, u32[]{:S(2)}) copy-start(f32[8,768]{1,0:T(8,128)} %param.15) | copy-start | bytes 73732
  206.1 16.7 %all-to-all-start.6 = ((bf16[128,2,768]{2,1,0:T(2,128)(2,1)}), bf16[128,2,768]{2,1,0:T(2,128)(2,1)S(1)}, u32[]{:S(2)}, u32[]{:S(2)}) async-start(bf16[128,2,768]{2,1,0:T(2,128)(2,1)} %reshape.229), calls=%async_computation.6 | async-start | bytes 786432 | tf_op jit(solution)/shard_map/all_to_all | solution.py:22
  489.8 16.7 %all-to-all-start.12 = ((bf16[128,2,768]{2,1,0:T(2,128)(2,1)}), bf16[128,2,768]{2,1,0:T(2,128)(2,1)S(1)}, u32[]{:S(2)}, u32[]{:S(2)}) async-start(bf16[128,2,768]{2,1,0:T(2,128)(2,1)} %reshape.253), calls=%async_computation.12 | async-start | bytes 786432 | tf_op jit(solution)/shard_map/all_to_all | solution.py:22
where the time goes:
time: 576 us; the launch traced here: 567 us
  blocking collectives  317 us (55%)
  matrix products  134 us (23%)
  between operations  39.4 us (7%)
  waiting for transfers between devices  32 us (6%)
  local copies, waits for them, and re-layouts  21.6 us (4%)
  starting transfers between devices  14.5 us (3%)
  other arithmetic  7.59 us (1%)
    psum x20, blocking collectives, over_axes(): array = lax.psum(array, axis)  150 us
    all_to_all x9, blocking collectives, transport(): lax.all_to_all(buffer.reshape(devices, capacity, breadth), FLUID_SOLID, s...  147 us
    dot_general x6, matrix products, per_device(): jnp.einsum('bcj,bij->bci', displaced.reshape(blocks, 3, nodes), rbf_block...  50.9 us
    dot_general x6, matrix products, per_device(): jnp.einsum('bci,bij->bcj', load.reshape(blocks, 3, nodes), rbf_blocks, pr...  40.5 us
    all_to_all x3, waiting for transfers between devices, transport(): lax.all_to_all(buffer.reshape(devices, capacity, breadth), FLUID_SOLID, s...  32 us
    dot_general x6, matrix products, per_device(): jnp.einsum('bi,bij->bj', forcing, shell_inverse, preferred_element_type=j...  30.1 us
    all_to_all x1, blocking collectives, per_device(): lax.all_to_all(wanted.reshape(devices, capacity), FLUID_SOLID, split_axis...  20 us
    all_to_all x3, starting transfers between devices, transport(): lax.all_to_all(buffer.reshape(devices, capacity, breadth), FLUID_SOLID, s...  14.5 us
  transfers between devices with their start and end apart: 3, of which 3 were waited for; matrix products, arithmetic and copies ran while one was open for 1% of the time, Pallas kernels for 0%

commit v1 on v0

--- a/solution.py
+++ b/solution.py
@@ -13,7 +13,7 @@
 
 def over_axes(array, axes):
     for axis in axes:
-        array = lax.psum(array, axis)
+        array = jnp.sum(lax.all_gather(array, axis), axis=0)
     return array
 
 

time: 576 us -> 779 us (1.35)
  blocking collectives: 317 us -> 403 us
  local copies, waits for them, and re-layouts: 21.6 us -> 76.3 us
  other arithmetic: 7.59 us -> 27.5 us
  waiting for transfers between devices: 32 us -> 49.8 us
  starting transfers between devices: 14.5 us -> 28.9 us
  between operations: 39.4 us -> 49.4 us
    psum x20 -> x0, blocking collectives: 150 us -> none  [over_axes(): array = lax.psum(array, axis)]
    unnamed x0 -> x20, blocking collectives: none -> 148 us
    all_gather x0 -> x16, blocking collectives: none -> 129 us  [over_axes(): array = jnp.sum(lax.all_gather(array, axis), axis=0)]
    unnamed x16 -> x124, local copies, waits for them, and re-layouts: 3.25 us -> 54.2 us
    all_to_all x9 -> x6, blocking collectives: 147 us -> 106 us  [transport(): lax.all_to_all(buffer.reshape(devices, capacity, breadth), FLUID_SOLID, s...]
    reduce_sum x0 -> x64, other arithmetic: none -> 20 us  [over_axes(): array = jnp.sum(lax.all_gather(array, axis), axis=0)]
    all_to_all x3 -> x6, waiting for transfers between devices: 32 us -> 49.8 us  [transport(): lax.all_to_all(buffer.reshape(devices, capacity, breadth), FLUID_SOLID, s...]
    all_to_all x3 -> x6, starting transfers between devices: 14.5 us -> 28.9 us  [transport(): lax.all_to_all(buffer.reshape(devices, capacity, breadth), FLUID_SOLID, s...]
  transfers between devices with their start and end apart: 3 -> 6, of which waited for: 3 -> 6; matrix products, arithmetic and copies ran while one was open for 1% -> 1% of each run, Pallas kernels for 0% -> 0%
where the time goes in v1:
time: 779 us; the launch traced here: 769 us
  blocking collectives  403 us (52%)
  matrix products  134 us (17%)
  local copies, waits for them, and re-layouts  76.3 us (10%)
  waiting for transfers between devices  49.8 us (6%)
  between operations  49.4 us (6%)
  starting transfers between devices  28.9 us (4%)
  other arithmetic  27.5 us (4%)
    unnamed x20, blocking collectives  148 us
    all_gather x16, blocking collectives, over_axes(): array = jnp.sum(lax.all_gather(array, axis), axis=0)  129 us
    all_to_all x6, blocking collectives, transport(): lax.all_to_all(buffer.reshape(devices, capacity, breadth), FLUID_SOLID, s...  106 us
    unnamed x124, local copies, waits for them, and re-layouts  54.2 us
    dot_general x6, matrix products, per_device(): jnp.einsum('bcj,bij->bci', displaced.reshape(blocks, 3, nodes), rbf_block...  50.9 us
    all_to_all x6, waiting for transfers between devices, transport(): lax.all_to_all(buffer.reshape(devices, capacity, breadth), FLUID_SOLID, s...  49.8 us
    dot_general x6, matrix products, per_device(): jnp.einsum('bci,bij->bcj', load.reshape(blocks, 3, nodes), rbf_blocks, pr...  40.5 us
    dot_general x6, matrix products, per_device(): jnp.einsum('bi,bij->bj', forcing, shell_inverse, preferred_element_type=j...  30.1 us
  transfers between devices with their start and end apart: 6, of which 6 were waited for; matrix products, arithmetic and copies ran while one was open for 1% of the time, Pallas kernels for 0%

profile of v1, /device:TPU:0, one launch (start us, length us, event | category | flops | bytes accessed | tf_op | source)
XLA Modules:
  0.0 768.8 jit_solution(12957888353246251935)
XLA Ops:
  2.5 20.0 %all_to_all.66 = s32[128,1,2]{2,1,0:T(1,128)S(1)} all-to-all(s32[128,1,2]{2,1,0:T(1,128)S(1)} %bitcast.439), channel_id=1, replica_groups=mesh['fluid_0'=4,'fluid_1'=4,'fluid_2'=2,'solid'=4] {'fluid_0','fluid_1'..., dimensions={0} | all-to-all | bytes 2048 | tf_op jit(solution)/shard_map/all_to_all | solution.py:81
  33.7 9.0 %all-to-all-done.1 = bf16[128,2,768]{2,1,0:T(2,128)(2,1)S(1)} async-done(((bf16[128,2,768]{2,1,0:T(2,128)(2,1)}), bf16[128,2,768]{2,1,0:T(2,128)(2,1)S(1)}, u32[]{:S(2)}, u32[]{:S(2)}) %all-to-all-start.1) | async-done | bytes 393248 | tf_op jit(solution)/shard_map/all_to_all | solution.py:22
  59.9 16.5 %all_to_all.67 = bf16[128,2,768]{2,1,0:T(2,128)(2,1)S(1)} all-to-all(bf16[128,2,768]{2,1,0:T(2,128)(2,1)S(1)} %reshape.229), channel_id=1, replica_groups=mesh['fluid_0'=4,'fluid_1'=4,'fluid_2'=2,'solid'=4] {'fluid_0','fluid_1'..., dimensions={0} | all-to-all | bytes 786432 | tf_op jit(solution)/shard_map/all_to_all | solution.py:22
  82.3 16.8 %all_to_all.68 = bf16[128,2,768]{2,1,0:T(2,128)(2,1)S(1)} all-to-all(bf16[128,2,768]{2,1,0:T(2,128)(2,1)S(1)} %reshape.231), channel_id=1, replica_groups=mesh['fluid_0'=4,'fluid_1'=4,'fluid_2'=2,'solid'=4] {'fluid_0','fluid_1'..., dimensions={0} | all-to-all | bytes 786432 | tf_op jit(solution)/shard_map/all_to_all | solution.py:22
  122.5 11.2 %all-to-all-done.4 = bf16[128,2,768]{2,1,0:T(2,128)(2,1)S(1)} async-done(((bf16[128,2,768]{2,1,0:T(2,128)(2,1)}), bf16[128,2,768]{2,1,0:T(2,128)(2,1)S(1)}, u32[]{:S(2)}, u32[]{:S(2)}) %all-to-all-start.4) | async-done | bytes 393248 | tf_op jit(solution)/shard_map/all_to_all | solution.py:22
  188.5 16.4 %all_to_all.69 = bf16[128,2,768]{2,1,0:T(2,128)(2,1)S(1)} all-to-all(bf16[128,2,768]{2,1,0:T(2,128)(2,1)S(1)} %reshape.238), channel_id=1, replica_groups=mesh['fluid_0'=4,'fluid_1'=4,'fluid_2'=2,'solid'=4] {'fluid_0','fluid_1'..., dimensions={0} | all-to-all | bytes 786432 | tf_op jit(solution)/shard_map/all_to_all | solution.py:22
  230.2 9.3 %all-to-all-done.6 = bf16[128,2,768]{2,1,0:T(2,128)(2,1)S(1)} async-done(((bf16[128,2,768]{2,1,0:T(2,128)(2,1)}), bf16[128,2,768]{2,1,0:T(2,128)(2,1)S(1)}, u32[]{:S(2)}, u32[]{:S(2)}) %all-to-all-start.6) | async-done | bytes 393248 | tf_op jit(solution)/shard_map/all_to_all | solution.py:22
  255.5 9.0 %all-reduce.9 = f32[8]{0:T(128)S(1)} all-reduce(f32[8]{0:T(128)S(1)} %dynamic-update-slice.9), channel_id=3, replica_groups=mesh['fluid_0'=4,'fluid_1'=4,'fluid_2'=2,'solid'=4] {'fluid_1'}, use_global_device_ids=true, to_apply=%add.9 | all-reduce | flops 8 | bytes 64
  307.8 16.0 %all_to_all.70 = bf16[128,2,768]{2,1,0:T(2,128)(2,1)S(1)} all-to-all(bf16[128,2,768]{2,1,0:T(2,128)(2,1)S(1)} %reshape.246), channel_id=1, replica_groups=mesh['fluid_0'=4,'fluid_1'=4,'fluid_2'=2,'solid'=4] {'fluid_0','fluid_1'..., dimensions={0} | all-to-all | bytes 786432 | tf_op jit(solution)/shard_map/all_to_all | solution.py:22
  349.2 9.3 %all-to-all-done.8 = bf16[128,2,768]{2,1,0:T(2,128)(2,1)S(1)} async-done(((bf16[128,2,768]{2,1,0:T(2,128)(2,1)}), bf16[128,2,768]{2,1,0:T(2,128)(2,1)S(1)}, u32[]{:S(2)}, u32[]{:S(2)}) %all-to-all-start.8) | async-done | bytes 393248 | tf_op jit(solution)/shard_map/all_to_all | solution.py:22
  396.5 10.4 %all-gather.36 = f32[4,3,3]{2,1,0:T(4,128)S(1)} all-gather(f32[1,3,3]{2,1,0:T(4,128)S(1)} %convolution_bitcast_fusion.2), channel_id=14, replica_groups=mesh['fluid_0'=4,'fluid_1'=4,'fluid_2'=2,'solid'=4] {'fluid_0'}, dimensions={0}, use_global_device_ids=true | all-gather | bytes 180 | tf_op jit(solution)/shard_map/all_gather | solution.py:16
  406.9 10.4 %all-gather.37 = f32[4,3,3]{2,1,0:T(4,128)S(1)} all-gather(f32[1,3,3]{2,1,0:T(4,128)S(1)} %bitcast.472), channel_id=15, replica_groups=mesh['fluid_0'=4,'fluid_1'=4,'fluid_2'=2,'solid'=4] {'fluid_1'}, dimensions={0}, use_global_device_ids=true | all-gather | bytes 180 | tf_op jit(solution)/shard_map/all_gather | solution.py:16
  419.1 10.4 %all-gather.39 = f32[4,3,3]{2,1,0:T(4,128)S(1)} all-gather(f32[1,3,3]{2,1,0:T(4,128)S(1)} %bitcast.470), channel_id=17, replica_groups=mesh['fluid_0'=4,'fluid_1'=4,'fluid_2'=2,'solid'=4] {'solid'}, dimensions={0}, use_global_device_ids=true | all-gather | bytes 180 | tf_op jit(solution)/shard_map/all_gather | solution.py:16
  437.0 20.0 %all_to_all.71 = bf16[128,2,768]{2,1,0:T(2,128)(2,1)S(1)} all-to-all(bf16[128,2,768]{2,1,0:T(2,128)(2,1)S(1)} %reshape.254), channel_id=1, replica_groups=mesh['fluid_0'=4,'fluid_1'=4,'fluid_2'=2,'solid'=4] {'fluid_0','fluid_1'..., dimensions={0} | all-to-all | bytes 786432 | tf_op jit(solution)/shard_map/all_to_all | solution.py:22
  482.3 9.3 %all-to-all-done.10 = bf16[128,2,768]{2,1,0:T(2,128)(2,1)S(1)} async-done(((bf16[128,2,768]{2,1,0:T(2,128)(2,1)}), bf16[128,2,768]{2,1,0:T(2,128)(2,1)S(1)}, u32[]{:S(2)}, u32[]{:S(2)}) %all-to-all-start.10) | async-done | bytes 393248 | tf_op jit(solution)/shard_map/all_to_all | solution.py:22
  529.6 10.4 %all-gather.40 = f32[4,4,4]{2,1,0:T(4,128)S(1)} all-gather(f32[1,4,4]{2,1,0:T(4,128)S(1)} %convolution_bitcast_fusion.1), channel_id=22, replica_groups=mesh['fluid_0'=4,'fluid_1'=4,'fluid_2'=2,'solid'=4] {'fluid_0'}, dimensions={0}, use_global_device_ids=true | all-gather | bytes 320 | tf_op jit(solution)/shard_map/all_gather | solution.py:16
  540.0 10.4 %all-gather.41 = f32[4,4,4]{2,1,0:T(4,128)S(1)} all-gather(f32[1,4,4]{2,1,0:T(4,128)S(1)} %bitcast.474), channel_id=23, replica_groups=mesh['fluid_0'=4,'fluid_1'=4,'fluid_2'=2,'solid'=4] {'fluid_1'}, dimensions={0}, use_global_device_ids=true | all-gather | bytes 320 | tf_op jit(solution)/shard_map/all_gather | solution.py:16
  552.2 10.4 %all-gather.43 = f32[4,4,4]{2,1,0:T(4,128)S(1)} all-gather(f32[1,4,4]{2,1,0:T(4,128)S(1)} %bitcast.471), channel_id=25, replica_groups=mesh['fluid_0'=4,'fluid_1'=4,'fluid_2'=2,'solid'=4] {'solid'}, dimensions={0}, use_global_device_ids=true | all-gather | bytes 320 | tf_op jit(solution)/shard_map/all_gather | solution.py:16
  573.5 20.1 %all_to_all.72 = bf16[128,2,768]{2,1,0:T(2,128)(2,1)S(1)} all-to-all(bf16[128,2,768]{2,1,0:T(2,128)(2,1)S(1)} %reshape.262), channel_id=1, replica_groups=mesh['fluid_0'=4,'fluid_1'=4,'fluid_2'=2,'solid'=4] {'fluid_0','fluid_1'..., dimensions={0} | all-to-all | bytes 786432 | tf_op jit(solution)/shard_map/all_to_all | solution.py:22
  657.8 9.9 %all-reduce.50 = (f32[20]{0:T(128)S(1)}, f32[4]{0:T(128)S(1)}, f32[4]{0:T(128)S(1)}, f32[4]{0:T(128)S(1)}, f32[4]{0:T(128)S(1)}, /*index=5*/f32[4]{0:T(128)S(1)}, f32[4]{0:T(128)S(1)}) all-reduce(f32[20]{0:T(128)S(1)} %dynamic-update-slice.21, ...), channel_id=27, replica_groups=mesh['fluid_0'=4,'fluid_1'=4,'fluid_2'=2,'solid'=4] {'fluid_1'}, use_global_device_ids=true, to_apply=%add.21 | all-reduce | flops 44 | bytes 352
  695.6 11.2 %all-reduce.48 = (f32[20]{0:T(128)S(1)}, f32[4]{0:T(128)S(1)}, f32[4]{0:T(128)S(1)}, f32[4]{0:T(128)S(1)}, f32[4]{0:T(128)S(1)}, /*index=5*/f32[4]{0:T(128)S(1)}, f32[4]{0:T(128)S(1)}) all-reduce(f32[20]{0:T(128)S(1)} %dynamic-update-slice.23, ...), channel_id=29, replica_groups=mesh['fluid_0'=4,'fluid_1'=4,'fluid_2'=2,'solid'=4] {'solid'}, use_global_device_ids=true, to_apply=%add.23 | all-reduce | flops 44 | bytes 352
  707.6 11.9 %all-gather.44 = f32[4,5,5]{2,1,0:T(8,128)S(1)} all-gather(f32[1,5,5]{2,1,0:T(8,128)S(1)} %convolution_bitcast_fusion), channel_id=30, replica_groups=mesh['fluid_0'=4,'fluid_1'=4,'fluid_2'=2,'solid'=4] {'fluid_0'}, dimensions={0}, use_global_device_ids=true | all-gather | bytes 500 | tf_op jit(solution)/shard_map/all_gather | solution.py:16
  719.5 11.9 %all-gather.45 = f32[4,5,5]{2,1,0:T(8,128)S(1)} all-gather(f32[1,5,5]{2,1,0:T(8,128)S(1)} %bitcast.468), channel_id=31, replica_groups=mesh['fluid_0'=4,'fluid_1'=4,'fluid_2'=2,'solid'=4] {'fluid_1'}, dimensions={0}, use_global_device_ids=true | all-gather | bytes 500 | tf_op jit(solution)/shard_map/all_gather | solution.py:16
  733.3 11.9 %all-gather.47 = f32[4,5,5]{2,1,0:T(8,128)S(1)} all-gather(f32[1,5,5]{2,1,0:T(8,128)S(1)} %bitcast.467), channel_id=33, replica_groups=mesh['fluid_0'=4,'fluid_1'=4,'fluid_2'=2,'solid'=4] {'solid'}, dimensions={0}, use_global_device_ids=true | all-gather | bytes 500 | tf_op jit(solution)/shard_map/all_gather | solution.py:16
  (394 shorter events, 417.3 us)
Async XLA Ops:
  25.9 16.8 %all-to-all-start.1 = ((bf16[128,2,768]{2,1,0:T(2,128)(2,1)}), bf16[128,2,768]{2,1,0:T(2,128)(2,1)S(1)}, u32[]{:S(2)}, u32[]{:S(2)}) async-start(bf16[128,2,768]{2,1,0:T(2,128)(2,1)} %reshape.224), calls=%async_computation.1 | async-start | bytes 786432 | tf_op jit(solution)/shard_map/all_to_all | solution.py:22
  52.1 24.4 %copy-start = (f32[8,768]{1,0:T(8,128)S(1)}, f32[8,768]{1,0:T(8,128)}, u32[]{:S(2)}) copy-start(f32[8,768]{1,0:T(8,128)} %param.14) | copy-start | bytes 73732
  52.2 24.4 %copy-start.1 = (f32[8,768]{1,0:T(8,128)S(1)}, f32[8,768]{1,0:T(8,128)}, u32[]{:S(2)}) copy-start(f32[8,768]{1,0:T(8,128)} %param.15) | copy-start | bytes 73732
  108.3 13.5 %copy-start.5 = (u32[128]{0:T(128)S(1)}, u32[128]{0:T(128)}, u32[]{:S(2)}) copy-start(u32[128]{0:T(128)} %constant.35) | copy-start | bytes 1540
  108.8 33.7 %copy-start.4 = (u32[128]{0:T(128)S(1)}, u32[128]{0:T(128)}, u32[]{:S(2)}) copy-start(u32[128]{0:T(128)} %constant.40) | copy-start | bytes 1540
  115.5 40.4 %copy-start.3 = (u32[128]{0:T(128)S(1)}, u32[128]{0:T(128)}, u32[]{:S(2)}) copy-start(u32[128]{0:T(128)} %constant.45) | copy-start | bytes 1540
  115.5 54.0 %copy-start.2 = (u32[128]{0:T(128)S(1)}, u32[128]{0:T(128)}, u32[]{:S(2)}) copy-start(u32[128]{0:T(128)} %constant.50) | copy-start | bytes 1540
  117.0 16.7 %all-to-all-start.4 = ((bf16[128,2,768]{2,1,0:T(2,128)(2,1)}), bf16[128,2,768]{2,1,0:T(2,128)(2,1)S(1)}, u32[]{:S(2)}, u32[]{:S(2)}) async-start(bf16[128,2,768]{2,1,0:T(2,128)(2,1)} %reshape.236), calls=%async_computation.4 | async-start | bytes 786432 | tf_op jit(solution)/shard_map/all_to_all | solution.py:22
  222.8 16.7 %all-to-all-start.6 = ((bf16[128,2,768]{2,1,0:T(2,128)(2,1)}), bf16[128,2,768]{2,1,0:T(2,128)(2,1)S(1)}, u32[]{:S(2)}, u32[]{:S(2)}) async-start(bf16[128,2,768]{2,1,0:T(2,128)(2,1)} %reshape.243), calls=%async_computation.6 | async-start | bytes 786432 | tf_op jit(solution)/shard_map/all_to_all | solution.py:22
  341.8 16.7 %all-to-all-start.8 = ((bf16[128,2,768]{2,1,0:T(2,128)(2,1)}), bf16[128,2,768]{2,1,0:T(2,128)(2,1)S(1)}, u32[]{:S(2)}, u32[]{:S(2)}) async-start(bf16[128,2,768]{2,1,0:T(2,128)(2,1)} %reshape.251), calls=%async_computation.8 | async-start | bytes 786432 | tf_op jit(solution)/shard_map/all_to_all | solution.py:22
  474.9 16.7 %all-to-all-start.10 = ((bf16[128,2,768]{2,1,0:T(2,128)(2,1)}), bf16[128,2,768]{2,1,0:T(2,128)(2,1)S(1)}, u32[]{:S(2)}, u32[]{:S(2)}) async-start(bf16[128,2,768]{2,1,0:T(2,128)(2,1)} %reshape.259), calls=%async_computation.10 | async-start | bytes 786432 | tf_op jit(solution)/shard_map/all_to_all | solution.py:22
  611.6 16.7 %all-to-all-start.12 = ((bf16[128,2,768]{2,1,0:T(2,128)(2,1)}), bf16[128,2,768]{2,1,0:T(2,128)(2,1)S(1)}, u32[]{:S(2)}, u32[]{:S(2)}) async-start(bf16[128,2,768]{2,1,0:T(2,128)(2,1)} %reshape.267), calls=%async_computation.12 | async-start | bytes 786432 | tf_op jit(solution)/shard_map/all_to_all | solution.py:22
